TPU v7x, 256 devices: a whole 4x4x8 slice. The times are simulated.
256 devices in a mesh: section: 32 (over z_lo, y, x), tp: 8 (over z_hi, core).
Axes of the slice: x: 4, y: 4, z: 8 (z_hi: 4, z_lo: 2; z = z_hi * 2 + z_lo), core: 2. Of those that a mesh axis runs over, the one named last changes fastest.
Arguments:
- prefill_hidden: bfloat16 [8192, 8192], P('section', 'tp'), may hold values from -180 to 180
- norm_gain: float32 [8192], replicated, may hold values from 0.25 to 1.75
- key_weight: bfloat16 [8192, 1024], P(None, 'tp'), may hold values from -0.0625 to 0.0625
- value_weight: bfloat16 [8192, 1024], P(None, 'tp'), may hold values from -0.0625 to 0.0625
- prefill_query: bfloat16 [8192, 8192], P('section', 'tp'), may hold values from -102 to 102
- resident_keys: bfloat16 [8192, 16, 1024], P('section', None, 'tp'), may hold values from -6 to 6
- resident_values: bfloat16 [8192, 16, 1024], P('section', None, 'tp'), may hold values from -6 to 6
- decode_query: bfloat16 [512, 8192], P('section', 'tp'), may hold values from -102 to 102
- page_owner: int32 [512], P('section'), may hold values from 0 to 31, as said below
- block_table: int32 [512, 64], P('section'), may hold values from 0 to 319, as said below
- context_len: int32 [512], P('section'), may hold values from 1 to 1024, as said below
Outputs:
- prefill_attention: bfloat16 [8192, 8192], P('section', 'tp')
- decode_attention: bfloat16 [512, 8192], P('section', 'tp')
Inputs may be any that keep to these rules, and one draw needn't show every extreme that they name: `page_owner`: the 16 pages of each section device go to 8 different owners, exactly 2 pages to each; one owner receives pages from every section device. `block_table`: row entries name first the row's resident pages (below 256), then 256 + page_slot for at most 4 pages sent to the row's owner; every page sent to an owner is named by exactly one of its rows; entries after a row's pages are 0. `context_len`: A row's last visible token lies in the last page its table names.
All inputs are finite; a program needn't handle non-finite values.
Results may differ from a plain program's by a relative error of at most 0.011.
Values may be sent and summed in bfloat16 or wider, within the bound.
A program may use at most 192 MiB of HBM per device.

v0:
```python
import math
import jax
import jax.numpy as jnp
from jax import lax
from jax.sharding import PartitionSpec as P

HD = 128
PAGE = 16
CAP = 2
NORM_EPSILON = 1e-05
ROPE_THETA = 500000.0
NEG_LARGE = -1e30


def rotate_keys(raw_keys, positions):
    head_width = raw_keys.shape[-1]
    half_width = head_width // 2
    frequency = jnp.exp(
        jnp.arange(half_width, dtype=jnp.float32) * (-2.0 * math.log(ROPE_THETA) / head_width)
    )
    angles = positions.astype(jnp.float32)[:, None] * frequency[None, :]
    cosine = jnp.cos(angles)[:, None, :]
    sine_part = jnp.sin(angles)[:, None, :]
    first_half = raw_keys[..., :half_width]
    second_half = raw_keys[..., half_width:]
    return jnp.concatenate(
        [
            first_half * cosine - second_half * sine_part,
            second_half * cosine + first_half * sine_part,
        ],
        axis=-1,
    )


def empty_state(kv_heads, group_size, query_rows, head_width):
    return (
        jnp.full((kv_heads, group_size, query_rows), NEG_LARGE, jnp.float32),
        jnp.zeros((kv_heads, group_size, query_rows), jnp.float32),
        jnp.zeros((kv_heads, group_size, query_rows, head_width), jnp.float32),
    )


def attend_piece(carried, queries, query_pos, key_piece, value_piece, key_pos, score_scale):
    kv_heads = queries.shape[1]
    head_width = queries.shape[3]

    def compute(current):
        row_max, row_sum, weighted = current
        piece_rows = key_piece.shape[0]
        key_block = key_piece.reshape(piece_rows, kv_heads, head_width)
        value_block = value_piece.reshape(piece_rows, kv_heads, head_width)
        scores = (
            jnp.einsum("tkgd,rkd->kgtr", queries, key_block, preferred_element_type=jnp.float32)
            * score_scale
        )
        visible = key_pos[None, :] <= query_pos[:, None]
        scores = jnp.where(visible, scores, NEG_LARGE)
        new_max = jnp.maximum(row_max, jnp.max(scores, axis=-1))
        weights = jnp.where(visible, jnp.exp(scores - new_max[..., None]), 0.0)
        new_sum = jnp.sum(weights, axis=-1)
        product = jnp.einsum(
            "kgtr,rkd->kgtd",
            weights.astype(jnp.bfloat16),
            value_block,
            preferred_element_type=jnp.float32,
        )
        return (new_max, new_sum, product)

    return lax.cond(
        jnp.min(key_pos) > jnp.max(query_pos), lambda current: current, compute, carried
    )


def finish_state(carried):
    row_max, row_sum, weighted = carried
    result = weighted / row_sum[..., None]
    kv_heads, group_size, query_rows, head_width = result.shape
    return (
        jnp.transpose(result, (2, 0, 1, 3))
        .reshape(query_rows, kv_heads * group_size * head_width)
        .astype(jnp.bfloat16)
    )


def per_device(
    prefill_hidden,
    norm_gain,
    key_weight,
    value_weight,
    prefill_query,
    resident_keys,
    resident_values,
    decode_query,
    page_owner,
    block_table,
    context_len,
):
    section_count = lax.axis_size("section")
    section_index = lax.axis_index("section")
    stretch_rows = prefill_hidden.shape[0]
    key_width = key_weight.shape[1]
    head_width = HD
    kv_heads = key_width // head_width
    query_width = prefill_query.shape[1]
    group_size = query_width // key_width
    score_scale = 1.0 / math.sqrt(head_width)
    features = lax.all_gather(prefill_hidden, "tp", axis=1, tiled=True)
    feature_f32 = features.astype(jnp.float32)
    inverse_rms = lax.rsqrt(
        jnp.mean(feature_f32 * feature_f32, axis=1, keepdims=True) + NORM_EPSILON
    )
    normed = (feature_f32 * inverse_rms * norm_gain).astype(jnp.bfloat16)
    raw_keys = jnp.dot(normed, key_weight, preferred_element_type=jnp.float32)
    value_rows = jnp.dot(normed, value_weight, preferred_element_type=jnp.float32).astype(
        jnp.bfloat16
    )
    positions = section_index * stretch_rows + jnp.arange(stretch_rows, dtype=jnp.int32)
    key_rows = (
        rotate_keys(raw_keys.reshape(stretch_rows, kv_heads, head_width), positions)
        .reshape(stretch_rows, key_width)
        .astype(jnp.bfloat16)
    )
    queries = prefill_query.reshape(stretch_rows, kv_heads, group_size, head_width)
    pieces = (
        lax.all_gather(key_rows, "section", axis=0, tiled=True),
        lax.all_gather(value_rows, "section", axis=0, tiled=True),
    )
    key_pos = jnp.arange(pieces[0].shape[0], dtype=jnp.int32)
    folded = attend_piece(
        empty_state(kv_heads, group_size, stretch_rows, head_width),
        queries,
        positions,
        pieces[0],
        pieces[1],
        key_pos,
        score_scale,
    )
    prefill_attention = finish_state(folded)
    pages_here = stretch_rows // PAGE
    page_data = jnp.concatenate([key_rows, value_rows], axis=1).reshape(
        pages_here, PAGE * 2 * key_width
    )
    page_index = jnp.arange(pages_here, dtype=jnp.int32)
    same_owner = (page_owner[:, None] == page_owner[None, :]) & (
        page_index[None, :] < page_index[:, None]
    )
    page_rank = jnp.sum(same_owner.astype(jnp.int32), axis=1)
    slot_index = page_owner * CAP + page_rank
    placement_matrix = (
        jnp.arange(section_count * CAP, dtype=jnp.int32)[:, None] == slot_index[None, :]
    ).astype(jnp.bfloat16)
    outgoing = jnp.dot(placement_matrix, page_data, preferred_element_type=jnp.float32).astype(
        jnp.bfloat16
    )
    outgoing = outgoing.reshape(section_count, CAP, PAGE * 2 * key_width)
    arrived = lax.all_to_all(outgoing, "section", split_axis=0, concat_axis=0, tiled=True).reshape(
        section_count * CAP, PAGE, 2 * key_width
    )
    cache_keys = jnp.concatenate([resident_keys, arrived[:, :, :key_width]], axis=0)
    cache_values = jnp.concatenate([resident_values, arrived[:, :, key_width:]], axis=0)
    decode_rows = decode_query.shape[0]
    key_span = block_table.shape[1] * PAGE
    gathered_keys = cache_keys[block_table].reshape(decode_rows, key_span, kv_heads, head_width)
    gathered_values = cache_values[block_table].reshape(decode_rows, key_span, kv_heads, head_width)
    decode_queries = decode_query.reshape(decode_rows, kv_heads, group_size, head_width)
    scores = (
        jnp.einsum(
            "bkgd,blkd->bkgl", decode_queries, gathered_keys, preferred_element_type=jnp.float32
        )
        * score_scale
    )
    visible = (jnp.arange(key_span, dtype=jnp.int32)[None, :] < context_len[:, None])[
        :, None, None, :
    ]
    scores = jnp.where(visible, scores, NEG_LARGE)
    row_max = jnp.max(scores, axis=-1, keepdims=True)
    weights = jnp.exp(scores - row_max)
    row_sum = jnp.sum(weights, axis=-1, keepdims=True)
    attended = (
        jnp.einsum(
            "bkgl,blkd->bkgd",
            weights.astype(jnp.bfloat16),
            gathered_values,
            preferred_element_type=jnp.float32,
        )
        / row_sum
    )
    decode_attention = attended.reshape(decode_rows, query_width).astype(jnp.bfloat16)
    return (prefill_attention, decode_attention)


def solution(mesh):
    return jax.shard_map(
        per_device,
        mesh=mesh,
        in_specs=(
            P("section", "tp"),
            P(),
            P(None, "tp"),
            P(None, "tp"),
            P("section", "tp"),
            P("section", None, "tp"),
            P("section", None, "tp"),
            P("section", "tp"),
            P("section"),
            P("section", None),
            P("section"),
        ),
        out_specs=(P("section", "tp"), P("section", "tp")),
        check_vma=False,
    )
```

profile of v0, /device:TPU:24, one launch (start us, length us, event | category | flops | bytes accessed | tf_op | source)
XLA Modules:
  0.0 413.2 jit_solution(1083435418822819909)
XLA Ops:
  7.2 0.0 copy-start
  7.2 0.0 copy-start.7
  7.2 0.0 all-gather.5.cloned.1.call-start
  7.2 0.7 all-gather.5.cloned.1.call-update
  7.9 0.0 all-gather.9.cloned.1.call-start
  8.0 56.6 %all-gather.5.cloned.1.call-done = bf16[256,8192]{1,0:T(8,128)(2,1)} async-done(((bf16[256,1024]{1,0:T(8,128)(2,1)}), bf16[256,8192]{1,0:T(8,128)(2,1)}) %all-gather.5.cloned.1.call-update) | async-done | bytes 4194320 | tf_op jit(solution)/shard_map/all_gather | solution.py:107
  64.6 0.0 copy-start.2
  64.6 3.3 fusion.20
  67.9 0.0 copy-done
  67.9 0.0 copy-done.7
  67.9 0.2 copy-done.2
  68.1 1.7 fusion.29
  69.8 0.3 fusion.46
  70.1 0.6 fusion.53
  70.8 0.0 all-gather.9.cloned.1.call-update
  70.8 0.0 copy-start.8
  70.8 0.0 copy-start.4
  70.8 0.0 copy-start.3
  70.8 0.0 copy-start.5
  70.8 0.0 all-gather.7.cloned.1.call-start
  70.9 5.2 %fusion.32 = bf16[256,128]{0,1:T(8,128)(2,1)} fusion(bf16[8192,128]{1,0:T(8,128)(2,1)} %param.16, bf16[256,8192]{1,0:T(8,128)(2,1)} %all-gather.5.cloned.1.call-done, f32[8192]{0:T(1024)S(1)} %copy-done.7, f32[256]{0:T(256)S(1)} %add_rsqrt_fusion), kind=kOutput, calls=%fused_computation.35 | convolution fusion | flops 545292288 | bytes 6390784 | tf_op jit(solution)/shard_map/dot_general | solution.py:114
  76.1 0.0 all-gather.7.cloned.1.call-update
  76.2 0.0 copy-done.8
  76.2 0.2 convert_reduce_fusion
  76.4 0.9 pad_maximum_fusion.2
  77.2 0.1 copy.30
  77.3 0.1 reshape.215
  77.4 0.3 convolution_convert_fusion
  77.7 1.1 reshape.216
  78.8 8.9 %all-to-all-start = ((bf16[32,2,4096]{2,1,0:T(2,128)(2,1)}), bf16[32,2,4096]{2,1,0:T(2,128)(2,1)S(1)}, u32[]{:S(2)}, u32[]{:S(2)}) async-start(bf16[32,2,4096]{2,1,0:T(2,128)(2,1)} %reshape.216), calls=%async_computation | async-start | bytes 1048576 | tf_op jit(solution)/shard_map/all_to_all | solution.py:156
  87.7 0.6 fusion.52
  88.4 0.0 copy-done.4
  88.4 0.1 reshape.223
  88.4 0.0 copy-done.3
  89.1 0.0 copy-done.5
  89.1 0.1 iota_compare_fusion
  89.2 9.3 %all-to-all-done = bf16[32,2,4096]{2,1,0:T(2,128)(2,1)S(1)} async-done(((bf16[32,2,4096]{2,1,0:T(2,128)(2,1)}), bf16[32,2,4096]{2,1,0:T(2,128)(2,1)S(1)}, u32[]{:S(2)}, u32[]{:S(2)}) %all-to-all-start) | async-done | bytes 524320 | tf_op jit(solution)/shard_map/all_to_all | solution.py:156
  98.5 0.3 reshape.217
  98.8 0.1 fusion.54
  98.9 2.8 pad_maximum_fusion
  101.8 9.6 %gather_fusion = bf16[1024,16,128]{2,1,0:T(8,128)(2,1)} fusion(bf16[320,16,128]{2,1,0:T(8,128)(2,1)} %get-tuple-element.49, s32[1024]{0:T(1024)S(1)} %broadcast_clamp_fusion), kind=kCustom, calls=%fused_computation | custom fusion | bytes 8392704 | tf_op jit(solution)/shard_map/gather | solution.py:163
  111.4 8.4 %gather_fusion.1 = bf16[1024,16,128]{2,1,0:T(8,128)(2,1)} fusion(bf16[320,16,128]{2,1,0:T(8,128)(2,1)S(1)} %get-tuple-element.50, s32[1024]{0:T(1024)S(1)} %broadcast_clamp_fusion), kind=kCustom, calls=%fused_computation.1 | custom fusion | bytes 8392704 | tf_op jit(solution)/shard_map/gather | solution.py:164
  119.7 0.0 copy-start.1
  119.7 0.0 copy-start.6
  119.7 3.6 fusion.55
  123.3 0.2 fusion.37
  123.6 0.0 copy-done.1
  123.6 0.7 fusion.35
  124.3 0.6 copy.49
  124.9 72.8 %all-gather.9.cloned.1.call-done = bf16[8192,1,128]{0,2,1:T(8,128)(2,1)} async-done(((bf16[256,1,128]{0,2,1:T(8,128)(2,1)}), bf16[8192,1,128]{0,2,1:T(8,128)(2,1)}) %all-gather.9.cloned.1.call-update) | async-done | bytes 2097168 | tf_op jit(solution)/shard_map/all_gather | solution.py:125
  197.7 127.6 %all-gather.7.cloned.1.call-done = bf16[8192,128]{0,1:T(8,128)(2,1)} async-done(((bf16[256,128]{0,1:T(8,128)(2,1)}), bf16[8192,128]{0,1:T(8,128)(2,1)}) %all-gather.7.cloned.1.call-update) | async-done | bytes 2097168 | tf_op jit(solution)/shard_map/all_gather | solution.py:126
  325.3 0.0 copy-done.6
  325.3 79.7 %conditional.1 = (f32[1,8,256]{2,1,0:T(8,128)S(1)}, f32[1,8,256,128]{3,2,1,0:T(8,128)S(1)}) conditional(s32[]{:T(128)} %convert_element_type.52, (s32[8192]{0:T(1024)S(1)}, s32[256]{0:T(256)S(1)}, bf16[256,1024]{1,0:T(8,128)(2,1)S(1)}, bf16[8192,128]{0,1:T(8,128)(2,1)}, bf16[8192,128]{0,1:T(8,128)(2,1)}) %tuple.37, () %tuple.17), branch_computations={%region_2.5_spmd, %region_5.0_spmd} | conditional | flops 8810133504 | bytes 215565328 | solution.py:69
  325.4 4.7 %broadcast_compare_fusion = pred[256,8192]{0,1:T(8,128)(4,1)} fusion(s32[256]{0:T(256)S(1)} %get-tuple-element.12, s32[8192]{0:T(1024)S(1)} %get-tuple-element.11), kind=kLoop, calls=%fused_computation.10 | loop fusion | flops 2097152 | bytes 2130944 | tf_op jit(solution)/shard_map/cond/branch_0_fun/le | solution.py:56
  330.0 25.5 %fusion = (f32[8,256]{1,0:T(8,128)S(1)}, f32[8192,256,8]{1,0,2:T(8,128)}) fusion(pred[256,8192]{0,1:T(8,128)(4,1)} %broadcast_compare_fusion, bf16[8192,128]{0,1:T(8,128)(2,1)} %get-tuple-element.37, bf16[256,1024]{1,0:T(8,128)(2,1)S(1)} %get-tuple-element.23), kind=kOutput, calls=%fused_computation.4 | convolution fusion | flops 4345296896 | bytes 71835648 | tf_op jit(solution)/shard_map/cond/branch_0_fun/tkgd,rkd->kgtr/dot_general | solution.py:53
  355.6 27.2 %fusion.10 = f32[1,8,256,128]{3,2,1,0:T(8,128)S(1)} fusion(bf16[8192,128]{0,1:T(8,128)(2,1)} %get-tuple-element.38, f32[8192,256,8]{1,0,2:T(8,128)} %get-tuple-element.40, f32[8,256]{1,0:T(8,128)S(1)} %broadcast_maximum_fusion, pred[256,8192]{0,1:T(8,128)(4,1)} %broadcast_compare_fusion), kind=kOutput, calls=%fused_computation.14 | convolution fusion | flops 4378853376 | bytes 72359936 | tf_op jit(solution)/shard_map/cond/branch_0_fun/kgtr,rkd->kgtd/dot_general | solution.py:61
  382.8 22.3 %fusion.2 = f32[8,256]{1,0:T(8,128)S(1)} fusion(f32[8192,256,8]{1,0,2:T(8,128)} %get-tuple-element.40, f32[8,256]{1,0:T(8,128)S(1)} %broadcast_maximum_fusion, pred[256,8192]{0,1:T(8,128)(4,1)} %broadcast_compare_fusion), kind=kLoop, calls=%fused_computation.6 | loop fusion | flops 83884032 | bytes 69222400 | tf_op jit(solution)/shard_map/cond/branch_0_fun/reduce_sum | solution.py:60
  405.0 0.3 fusion.36
  405.4 0.3 copy.29
  405.7 0.9 copy.48
  (10 shorter events, 0.1 us)
Async XLA Ops:
  7.2 60.7 %copy-start = (bf16[8192,128]{1,0:T(8,128)(2,1)S(1)}, bf16[8192,128]{1,0:T(8,128)(2,1)}, u32[]{:S(2)}) copy-start(bf16[8192,128]{1,0:T(8,128)(2,1)} %param.15) | copy-start | bytes 6291460
  7.2 60.7 %copy-start.7 = (f32[8192]{0:T(1024)S(1)}, f32[8192]{0:T(1024)}, u32[]{:S(2)}) copy-start(f32[8192]{0:T(1024)} %param.14) | copy-start | bytes 98308
  7.2 57.4 %all-gather.5.cloned.1.call-start = ((), (), s32[]{:S(2)}) async-start(), calls=%async_computation.1 | async-start | bytes 4718592 | tf_op jit(solution)/shard_map/all_gather | solution.py:107
  7.9 189.8 %all-gather.9.cloned.1.call-start = ((), (), s32[]{:S(2)}) async-start(), calls=%async_computation.3 | async-start | bytes 2162688 | tf_op jit(solution)/shard_map/all_gather | solution.py:125
  64.6 3.4 copy-start.2
  70.8 5.4 %copy-start.8 = (s32[16]{0:T(128)S(1)}, s32[16]{0:T(128)}, u32[]{:S(2)}) copy-start(s32[16]{0:T(128)} %param.21) | copy-start | bytes 196
  70.8 17.6 %copy-start.4 = (s32[16,64]{1,0:T(8,128)S(1)}, s32[16,64]{1,0:T(8,128)}, u32[]{:S(2)}) copy-start(s32[16,64]{1,0:T(8,128)} %param.22) | copy-start | bytes 12292
  70.8 17.6 %copy-start.3 = (bf16[16,1024]{1,0:T(8,128)(2,1)S(1)}, bf16[16,1024]{1,0:T(8,128)(2,1)}, u32[]{:S(2)}) copy-start(bf16[16,1024]{1,0:T(8,128)(2,1)} %param.20) | copy-start | bytes 98308
  70.8 18.3 %copy-start.5 = (s32[16]{0:T(128)S(1)}, s32[16]{0:T(128)}, u32[]{:S(2)}) copy-start(s32[16]{0:T(128)} %param.23) | copy-start | bytes 196
  70.8 254.5 %all-gather.7.cloned.1.call-start = ((), (), s32[]{:S(2)}) async-start(), calls=%async_computation.2 | async-start | bytes 2162688 | tf_op jit(solution)/shard_map/all_gather | solution.py:126
  78.8 19.7 %all-to-all-start = ((bf16[32,2,4096]{2,1,0:T(2,128)(2,1)}), bf16[32,2,4096]{2,1,0:T(2,128)(2,1)S(1)}, u32[]{:S(2)}, u32[]{:S(2)}) async-start(bf16[32,2,4096]{2,1,0:T(2,128)(2,1)} %reshape.216), calls=%async_computation | async-start | bytes 1048576 | tf_op jit(solution)/shard_map/all_to_all | solution.py:156
  119.7 3.8 copy-start.1
  119.7 205.6 %copy-start.6 = (bf16[256,1024]{1,0:T(8,128)(2,1)S(1)}, bf16[256,1024]{1,0:T(8,128)(2,1)}, u32[]{:S(2)}) copy-start(bf16[256,1024]{1,0:T(8,128)(2,1)} %param.17) | copy-start | bytes 1572868
Sparse Core Ops, SparseCore 0:
  9.8 54.7 all-gather.4
  70.9 126.7 all-gather.8
  199.4 125.8 all-gather.6
where the time goes:
time: 413 us
  waiting for transfers between devices  267 us (65%)
  matrix products  64.3 us (16%)
  other arithmetic  36.3 us (9%)
  local copies, waits for them, and re-layouts  21.9 us (5%)
  between operations  14.6 us (4%)
  starting transfers between devices  9.03 us (2%)
    all_gather x1, waiting for transfers between devices, per_device(): lax.all_gather(value_rows, 'section', axis=0, tiled=True)  128 us
    all_gather x1, waiting for transfers between devices, per_device(): lax.all_gather(key_rows, 'section', axis=0, tiled=True)  72.8 us
    all_gather x1, waiting for transfers between devices, per_device(): features = lax.all_gather(prefill_hidden, 'tp', axis=1, tiled=True)  56.6 us
    dot_general x1, matrix products, compute(): jnp.einsum('kgtr,rkd->kgtd', weights.astype(jnp.bfloat16), value_block, p...  27.2 us
    dot_general x1, matrix products, compute(): jnp.einsum('tkgd,rkd->kgtr', queries, key_block, preferred_element_type=j...  25.5 us
    reduce_sum x1, other arithmetic, compute(): new_sum = jnp.sum(weights, axis=-1)  22.3 us
    gather x1, local copies, waits for them, and re-layouts, per_device(): cache_keys[block_table].reshape(decode_rows, key_span, kv_heads, head_width)  9.61 us
    all_to_all x1, waiting for transfers between devices, per_device(): lax.all_to_all(outgoing, 'section', split_axis=0, concat_axis=0, tiled=True)  9.27 us
  transfers between devices with their start and end apart: 4, of which 4 were waited for; matrix products, arithmetic and copies ran while one was open for 8% of the time, Pallas kernels for 0%

commit v1 on v0

--- a/solution.py
+++ b/solution.py
@@ -123,7 +123,10 @@
     queries = prefill_query.reshape(stretch_rows, kv_heads, group_size, head_width)
     pieces = (
         lax.all_gather(key_rows, "section", axis=0, tiled=True),
-        lax.all_gather(value_rows, "section", axis=0, tiled=True),
+        jnp.concatenate(
+            lax.all_to_all(jnp.stack([value_rows] * lax.axis_size("section")), "section", 0, 0),
+            axis=0,
+        ),
     )
     key_pos = jnp.arange(pieces[0].shape[0], dtype=jnp.int32)
     folded = attend_piece(

time: 413 us -> 310 us (0.75)
  waiting for transfers between devices: 267 us -> 157 us
  starting transfers between devices: 9.03 us -> 14.9 us
    all_gather x1 -> x0, waiting for transfers between devices: 128 us -> none  [per_device(): lax.all_gather(value_rows, 'section', axis=0, tiled=True)]
    all_gather x1, waiting for transfers between devices: 72.8 us -> 91 us  [per_device(): lax.all_gather(key_rows, 'section', axis=0, tiled=True)]
    all_to_all x0 -> x1, starting transfers between devices: none -> 5.87 us  [per_device(): lax.all_to_all(jnp.stack([value_rows] * lax.axis_size('section')), 'secti...]
  transfers between devices with their start and end apart: 4 -> 4, of which waited for: 4 -> 3; matrix products, arithmetic and copies ran while one was open for 8% -> 10% of each run, Pallas kernels for 0% -> 0%
where the time goes in v1:
time: 310 us; the launch traced here: 309 us
  waiting for transfers between devices  157 us (51%)
  matrix products  60.6 us (20%)
  other arithmetic  36.9 us (12%)
  local copies, waits for them, and re-layouts  23.9 us (8%)
  starting transfers between devices  14.9 us (5%)
  between operations  14.9 us (5%)
    all_gather x1, waiting for transfers between devices, per_device(): lax.all_gather(key_rows, 'section', axis=0, tiled=True)  91 us
    all_gather x1, waiting for transfers between devices, per_device(): features = lax.all_gather(prefill_hidden, 'tp', axis=1, tiled=True)  55.1 us
    dot_general x1, matrix products, compute(): jnp.einsum('kgtr,rkd->kgtd', weights.astype(jnp.bfloat16), value_block, p...  27.1 us
    dot_general x1, matrix products, compute(): jnp.einsum('tkgd,rkd->kgtr', queries, key_block, preferred_element_type=j...  25.5 us
    reduce_sum x1, other arithmetic, compute(): new_sum = jnp.sum(weights, axis=-1)  22.3 us
    all_to_all x1, waiting for transfers between devices, per_device(): lax.all_to_all(outgoing, 'section', split_axis=0, concat_axis=0, tiled=True)  9.98 us
    gather x1, local copies, waits for them, and re-layouts, per_device(): cache_keys[block_table].reshape(decode_rows, key_span, kv_heads, head_width)  9.64 us
    all_to_all x1, starting transfers between devices, per_device(): lax.all_to_all(outgoing, 'section', split_axis=0, concat_axis=0, tiled=True)  8.91 us
  transfers between devices with their start and end apart: 4, of which 3 were waited for; matrix products, arithmetic and copies ran while one was open for 10% of the time, Pallas kernels for 0%

profile of v1, /device:TPU:24, one launch (start us, length us, event | category | flops | bytes accessed | tf_op | source)
XLA Modules:
  0.0 308.8 jit_solution(10768335590187252116)
XLA Ops:
  7.2 0.0 copy-start
  7.2 0.0 copy-start.8
  7.2 0.0 all-gather.4.cloned.1.call-start
  7.2 0.7 all-gather.4.cloned.1.call-update
  8.0 0.9 convert_reduce_fusion
  8.9 0.7 multiply_add_fusion
  9.5 55.1 %all-gather.4.cloned.1.call-done = bf16[256,8192]{1,0:T(8,128)(2,1)} async-done(((bf16[256,1024]{1,0:T(8,128)(2,1)}), bf16[256,8192]{1,0:T(8,128)(2,1)}) %all-gather.4.cloned.1.call-update) | async-done | bytes 4194320 | tf_op jit(solution)/shard_map/all_gather | solution.py:107
  64.6 0.0 copy-start.2
  64.6 3.3 %fusion.17 = f32[256]{0:T(256)S(1)} fusion(bf16[256,8192]{1,0:T(8,128)(2,1)} %all-gather.4.cloned.1.call-done), kind=kLoop, calls=%fused_computation.22 | loop fusion | flops 6291200 | bytes 4195328 | tf_op jit(solution)/shard_map/reduce_sum | solution.py:110
  67.9 0.0 copy-done
  67.9 0.0 copy-done.8
  67.9 0.2 copy-done.2
  68.1 0.0 copy-start.6
  68.1 1.7 fusion.26
  69.8 0.3 fusion.43
  70.1 0.6 fusion.50
  70.8 0.0 copy-done.6
  70.8 1.7 fusion.29
  72.5 0.1 copy.30
  72.7 0.1 reshape.218
  72.7 0.3 convolution_convert_fusion
  73.0 0.0 copy-start.4
  73.0 0.0 copy-start.3
  73.0 0.0 copy-start.5
  73.0 1.1 reshape.219
  74.2 8.9 %all-to-all-start.1 = ((bf16[32,2,4096]{2,1,0:T(2,128)(2,1)}), bf16[32,2,4096]{2,1,0:T(2,128)(2,1)S(1)}, u32[]{:S(2)}, u32[]{:S(2)}) async-start(bf16[32,2,4096]{2,1,0:T(2,128)(2,1)} %reshape.219), calls=%async_computation.1 | async-start | bytes 1048576 | tf_op jit(solution)/shard_map/all_to_all | solution.py:159
  83.1 0.0 all-gather.6.cloned.1.call-start
  83.1 0.1 copy.27
  83.3 0.6 all-gather.6.cloned.1.call-update
  83.8 10.0 %all-to-all-done.1 = bf16[32,2,4096]{2,1,0:T(2,128)(2,1)S(1)} async-done(((bf16[32,2,4096]{2,1,0:T(2,128)(2,1)}), bf16[32,2,4096]{2,1,0:T(2,128)(2,1)S(1)}, u32[]{:S(2)}, u32[]{:S(2)}) %all-to-all-start.1) | async-done | bytes 524320 | tf_op jit(solution)/shard_map/all_to_all | solution.py:159
  93.8 1.8 stack.2
  95.7 5.9 %all-to-all-start = ((bf16[32,256,128]{2,1,0:T(8,128)(2,1)}), bf16[32,256,128]{2,1,0:T(8,128)(2,1)}, u32[]{:S(2)}, u32[]{:S(2)}) async-start(bf16[32,256,128]{2,1,0:T(8,128)(2,1)} %stack.2), calls=%async_computation | async-start | bytes 4194304 | tf_op jit(solution)/shard_map/all_to_all | solution.py:127
  101.5 0.6 fusion.49
  102.2 0.0 copy-done.4
  102.2 0.1 reshape.226
  102.3 0.0 copy-done.3
  102.9 0.0 copy-done.5
  103.0 0.1 iota_compare_fusion
  103.0 0.3 reshape.220
  103.4 0.1 fusion.51
  103.5 2.8 pad_maximum_fusion
  106.3 9.6 %gather_fusion = bf16[1024,16,128]{2,1,0:T(8,128)(2,1)} fusion(bf16[320,16,128]{2,1,0:T(8,128)(2,1)} %get-tuple-element.49, s32[1024]{0:T(1024)S(1)} %broadcast_clamp_fusion), kind=kCustom, calls=%fused_computation | custom fusion | bytes 8392704 | tf_op jit(solution)/shard_map/gather | solution.py:166
  116.0 8.4 %gather_fusion.1 = bf16[1024,16,128]{2,1,0:T(8,128)(2,1)} fusion(bf16[320,16,128]{2,1,0:T(8,128)(2,1)S(1)} %get-tuple-element.50, s32[1024]{0:T(1024)S(1)} %broadcast_clamp_fusion), kind=kCustom, calls=%fused_computation.1 | custom fusion | bytes 8392704 | tf_op jit(solution)/shard_map/gather | solution.py:167
  124.3 0.0 copy-start.1
  124.3 0.0 copy-start.7
  124.3 3.6 %fusion.52 = (f32[16,8]{1,0:T(8,128)S(1)}, f32[16,8,1024]{2,1,0:T(8,128)S(1)}) fusion(bf16[16,1024,128]{2,1,0:T(8,128)(2,1)} %bitcast.74, bf16[16,8,128]{2,1,0:T(8,128)(2,1)S(1)} %bitcast.77, pred[16,1024]{1,0:T(8,128)(4,1)S(1)} %iota_compare_fusion), kind=kOutput, calls=%fused_computation.73 | convolution fusion | flops 33947520 | bytes 4768256 | tf_op jit(solution)/shard_map/bkgd,blkd->bkgl/dot_general | solution.py:170
  127.9 0.2 fusion.34
  128.2 0.0 copy-done.1
  128.2 0.7 fusion.32
  128.9 0.6 copy.47
  129.5 91.0 %all-gather.6.cloned.1.call-done = bf16[8192,1,128]{0,2,1:T(8,128)(2,1)} async-done(((bf16[256,1,128]{0,2,1:T(8,128)(2,1)}), bf16[8192,1,128]{0,2,1:T(8,128)(2,1)}) %all-gather.6.cloned.1.call-update) | async-done | bytes 2097168 | tf_op jit(solution)/shard_map/all_gather | solution.py:125
  220.5 0.0 all-to-all-done
  220.6 0.0 copy-done.7
  220.6 79.8 %conditional.1 = (f32[1,8,256]{2,1,0:T(8,128)S(1)}, f32[1,8,256,128]{3,2,1,0:T(8,128)S(1)}) conditional(s32[]{:T(128)} %convert_element_type.52, (s32[8192]{0:T(1024)S(1)}, s32[256]{0:T(256)S(1)}, bf16[256,1024]{1,0:T(8,128)(2,1)S(1)}, bf16[8192,128]{0,1:T(8,128)(2,1)}, bf16[32,256,128]{2,1,0:T(8,128)(2,1)}) %tuple.35, () %tuple.17), branch_computations={%region_2.5_spmd, %region_5.0_spmd} | conditional | flops 8810133504 | bytes 215565328 | solution.py:69
  220.8 4.7 %broadcast_compare_fusion = pred[256,8192]{0,1:T(8,128)(4,1)} fusion(s32[256]{0:T(256)S(1)} %get-tuple-element.12, s32[8192]{0:T(1024)S(1)} %get-tuple-element.11), kind=kLoop, calls=%fused_computation.10 | loop fusion | flops 2097152 | bytes 2130944 | tf_op jit(solution)/shard_map/cond/branch_0_fun/le | solution.py:56
  225.5 25.5 %fusion = (f32[8,256]{1,0:T(8,128)S(1)}, f32[8192,256,8]{1,0,2:T(8,128)}) fusion(pred[256,8192]{0,1:T(8,128)(4,1)} %broadcast_compare_fusion, bf16[8192,128]{0,1:T(8,128)(2,1)} %get-tuple-element.37, bf16[256,1024]{1,0:T(8,128)(2,1)S(1)} %get-tuple-element.23), kind=kOutput, calls=%fused_computation.4 | convolution fusion | flops 4345296896 | bytes 71835648 | tf_op jit(solution)/shard_map/cond/branch_0_fun/tkgd,rkd->kgtr/dot_general | solution.py:53
  251.0 27.1 %fusion.9 = f32[1,8,256,128]{3,2,1,0:T(8,128)S(1)} fusion(bf16[8192,128,1]{1,0,2:T(8,128)(2,1)} %bitcast.6, f32[8192,256,8]{1,0,2:T(8,128)} %get-tuple-element.40, f32[8,256]{1,0:T(8,128)S(1)} %broadcast_maximum_fusion, pred[256,8192]{0,1:T(8,128)(4,1)} %broadcast_compare_fusion), kind=kOutput, calls=%fused_computation.13 | convolution fusion | flops 4378853376 | bytes 72359936 | tf_op jit(solution)/shard_map/cond/branch_0_fun/kgtr,rkd->kgtd/dot_general | solution.py:61
  278.1 22.3 %fusion.2 = f32[8,256]{1,0:T(8,128)S(1)} fusion(f32[8192,256,8]{1,0,2:T(8,128)} %get-tuple-element.40, f32[8,256]{1,0:T(8,128)S(1)} %broadcast_maximum_fusion, pred[256,8192]{0,1:T(8,128)(4,1)} %broadcast_compare_fusion), kind=kLoop, calls=%fused_computation.6 | loop fusion | flops 83884032 | bytes 69222400 | tf_op jit(solution)/shard_map/cond/branch_0_fun/reduce_sum | solution.py:60
  300.3 0.3 fusion.33
  300.7 0.3 copy.29
  301.0 0.9 copy.46
  (10 shorter events, 0.1 us)
Async XLA Ops:
  7.2 60.7 %copy-start = (bf16[8192,128]{1,0:T(8,128)(2,1)S(1)}, bf16[8192,128]{1,0:T(8,128)(2,1)}, u32[]{:S(2)}) copy-start(bf16[8192,128]{1,0:T(8,128)(2,1)} %param.15) | copy-start | bytes 6291460
  7.2 60.7 %copy-start.8 = (f32[8192]{0:T(1024)S(1)}, f32[8192]{0:T(1024)}, u32[]{:S(2)}) copy-start(f32[8192]{0:T(1024)} %param.14) | copy-start | bytes 98308
  7.2 57.4 %all-gather.4.cloned.1.call-start = ((), (), s32[]{:S(2)}) async-start(), calls=%async_computation.2 | async-start | bytes 4718592 | tf_op jit(solution)/shard_map/all_gather | solution.py:107
  64.6 3.4 %copy-start.2 = (bf16[256,8192]{1,0:T(8,128)(2,1)S(1)}, bf16[256,8192]{1,0:T(8,128)(2,1)}, u32[]{:S(2)}) copy-start(bf16[256,8192]{1,0:T(8,128)(2,1)} %all-gather.4.cloned.1.call-done) | copy-start | bytes 12582916
  68.1 2.7 copy-start.6
  73.0 29.2 %copy-start.4 = (s32[16,64]{1,0:T(8,128)S(1)}, s32[16,64]{1,0:T(8,128)}, u32[]{:S(2)}) copy-start(s32[16,64]{1,0:T(8,128)} %param.22) | copy-start | bytes 12292
  73.0 29.2 %copy-start.3 = (bf16[16,1024]{1,0:T(8,128)(2,1)S(1)}, bf16[16,1024]{1,0:T(8,128)(2,1)}, u32[]{:S(2)}) copy-start(bf16[16,1024]{1,0:T(8,128)(2,1)} %param.20) | copy-start | bytes 98308
  73.0 29.9 %copy-start.5 = (s32[16]{0:T(128)S(1)}, s32[16]{0:T(128)}, u32[]{:S(2)}) copy-start(s32[16]{0:T(128)} %param.23) | copy-start | bytes 196
  74.2 19.7 %all-to-all-start.1 = ((bf16[32,2,4096]{2,1,0:T(2,128)(2,1)}), bf16[32,2,4096]{2,1,0:T(2,128)(2,1)S(1)}, u32[]{:S(2)}, u32[]{:S(2)}) async-start(bf16[32,2,4096]{2,1,0:T(2,128)(2,1)} %reshape.219), calls=%async_computation.1 | async-start | bytes 1048576 | tf_op jit(solution)/shard_map/all_to_all | solution.py:159
  83.1 137.5 %all-gather.6.cloned.1.call-start = ((), (), s32[]{:S(2)}) async-start(), calls=%async_computation.3 | async-start | bytes 2162688 | tf_op jit(solution)/shard_map/all_gather | solution.py:125
  95.7 124.9 %all-to-all-start = ((bf16[32,256,128]{2,1,0:T(8,128)(2,1)}), bf16[32,256,128]{2,1,0:T(8,128)(2,1)}, u32[]{:S(2)}, u32[]{:S(2)}) async-start(bf16[32,256,128]{2,1,0:T(8,128)(2,1)} %stack.2), calls=%async_computation | async-start | bytes 4194304 | tf_op jit(solution)/shard_map/all_to_all | solution.py:127
  124.3 3.8 %copy-start.1 = (bf16[1024,16,128]{2,1,0:T(8,128)(2,1)S(1)}, bf16[1024,16,128]{2,1,0:T(8,128)(2,1)}, u32[]{:S(2)}) copy-start(bf16[1024,16,128]{2,1,0:T(8,128)(2,1)} %gather_fusion.1) | copy-start | bytes 12582916
  124.3 96.2 %copy-start.7 = (bf16[256,1024]{1,0:T(8,128)(2,1)S(1)}, bf16[256,1024]{1,0:T(8,128)(2,1)}, u32[]{:S(2)}) copy-start(bf16[256,1024]{1,0:T(8,128)(2,1)} %param.17) | copy-start | bytes 1572868
Sparse Core Ops, SparseCore 0:
  9.8 54.7 all-gather.3
  85.6 134.8 all-gather.5
